TPU v7x, 256 devices: a whole 4x4x8 slice. The times are simulated.
256 devices in a mesh: req: 32 (over z_lo, x, core), tp: 8 (over z_hi, y).
Axes of the slice: x: 4, y: 4, z: 8 (z_hi: 2, z_lo: 4; z = z_hi * 4 + z_lo), core: 2. Of those that a mesh axis runs over, the one named last changes fastest.
Arguments:
- hidden: bfloat16 [8192, 4608], P('req', 'tp'), may hold values from -6 to 6
- norm_gain: float32 [4608], replicated, may hold values from 0.1 to 1.9
- w_query: bfloat16 [4608, 4096], P(None, 'tp'), may hold values from -0.25 to 0.25
- w_key: bfloat16 [4608, 2048], P(None, 'tp'), may hold values from -0.09375 to 0.09375
- w_value: bfloat16 [4608, 2048], P(None, 'tp'), may hold values from -0.09375 to 0.09375
- prefix_kv: bfloat16 [16384, 2, 2048], P('req', None, 'tp'), may hold values from -6 to 6
- group_of: int32 [32], replicated, may hold values from 0 to 3, as said below
- block_owner: int32 [4, 8], replicated, may hold values from 0 to 31, as said below
- lengths: int32 [32], replicated, may hold values from 32 to 256, as said below
Outputs:
- attended: bfloat16 [8192, 4096], P('req', 'tp')
- key_cache: bfloat16 [8192, 2048], P('req', 'tp')
- value_cache: bfloat16 [8192, 2048], P('req', 'tp')
Inputs may be any that keep to these rules, and one draw needn't show every extreme that they name: `group_of`: every group holds exactly 8 requests. `block_owner`: every block index appears exactly once. `lengths`: some request has exactly 256 live rows and some exactly 32.
All inputs are finite; a program needn't handle non-finite values.
Results may differ from a plain program's by a relative error of at most 0.011.
Values may be sent and summed in bfloat16 or wider, within the bound.
A program may use at most 256 MiB of HBM per device.

v0:
```python
import math
import jax
import jax.numpy as jnp
from jax import lax
from jax.sharding import PartitionSpec as P

HD = 128
GSIZE = 8
PREFIX = 4096
SOFTCAP = 50.0
EPSILON = 1e-06
QUERY_SCALE = 1.0 / 12.0


def rope_tables(positions, head_width):
    half_width = head_width // 2
    inverse_freq = jnp.exp(
        jnp.arange(half_width).astype(jnp.float32) * (-2.0 * math.log(10000.0) / head_width)
    )
    angles = positions.astype(jnp.float32)[:, None] * inverse_freq[None, :]
    return (jnp.cos(angles), jnp.sin(angles))


def rotate(values, cosine_table, sine_table):
    half_width = values.shape[-1] // 2
    lower_half = values[..., :half_width]
    upper_half = values[..., half_width:]
    cosine_part = cosine_table[:, None, :]
    sine_part = sine_table[:, None, :]
    return jnp.concatenate(
        [
            lower_half * cosine_part - upper_half * sine_part,
            upper_half * cosine_part + lower_half * sine_part,
        ],
        axis=-1,
    )


def attend(grouped, key_block, value_block, allowed_mask):
    scores = jnp.einsum("rkgd,ckd->kgrc", grouped, key_block, preferred_element_type=jnp.float32)
    weights = jnp.exp(SOFTCAP * jnp.tanh(scores / SOFTCAP))
    if allowed_mask is not None:
        weights = jnp.where(allowed_mask[None, None], weights, 0.0)
    denominator = jnp.transpose(jnp.sum(weights, axis=3), (2, 0, 1))
    numerator = jnp.einsum(
        "kgrc,ckd->rkgd",
        weights.astype(jnp.bfloat16),
        value_block,
        preferred_element_type=jnp.float32,
    )
    return (numerator, denominator)


def body(hidden, norm_gain, w_query, w_key, w_value, prefix_kv, group_of, block_owner, lengths):
    device = lax.axis_index("req")
    row_count = hidden.shape[0]
    gathered = lax.all_gather(hidden, "tp", axis=1, tiled=True)
    features = gathered.astype(jnp.float32)
    row_scale = lax.rsqrt(jnp.mean(features * features, axis=1, keepdims=True) + EPSILON)
    normed = (features * row_scale * norm_gain[None, :]).astype(jnp.bfloat16)
    heads_query = w_query.shape[1] // HD
    heads_kv = w_key.shape[1] // HD
    group_size = heads_query // heads_kv
    query_raw = jnp.dot(normed, w_query, preferred_element_type=jnp.float32)
    key_raw = jnp.dot(normed, w_key, preferred_element_type=jnp.float32)
    value_raw = jnp.dot(normed, w_value, preferred_element_type=jnp.float32)
    cosine_table, sine_table = rope_tables(jnp.arange(row_count) + PREFIX, HD)
    query_rows = (
        rotate(query_raw.reshape(row_count, heads_query, HD), cosine_table, sine_table)
        * QUERY_SCALE
    ).astype(jnp.bfloat16)
    live_rows = jnp.arange(row_count) < lengths[device]
    key_rows = jnp.where(
        live_rows[:, None, None],
        rotate(key_raw.reshape(row_count, heads_kv, HD), cosine_table, sine_table),
        0.0,
    ).astype(jnp.bfloat16)
    value_rows = jnp.where(live_rows[:, None], value_raw, 0.0).astype(jnp.bfloat16)
    grouped = query_rows.reshape(row_count, heads_kv, group_size, HD)
    causal = jnp.arange(row_count)[:, None] >= jnp.arange(row_count)[None, :]
    numerator, denominator = attend(
        grouped, key_rows, value_rows.reshape(row_count, heads_kv, HD), causal
    )
    device_count = lax.axis_size("req")
    flat_query = query_rows.reshape(row_count, heads_query * HD)
    everyone = lax.all_gather(flat_query, "req", axis=0, tiled=True)
    owned_group = jnp.sum(
        jnp.any(block_owner == device, axis=1).astype(jnp.int32)
        * jnp.arange(block_owner.shape[0], dtype=jnp.int32)
    )
    members = jnp.argsort((group_of != owned_group).astype(jnp.int32), stable=True)[:GSIZE]
    chosen = everyone.reshape(device_count, row_count, heads_kv, group_size, HD)[members]
    block_count = prefix_kv.shape[0]
    key_block = prefix_kv[:, 0].reshape(block_count, heads_kv, HD)
    value_block = prefix_kv[:, 1].reshape(block_count, heads_kv, HD)
    extra_num, extra_den = attend(
        chosen.reshape(GSIZE * row_count, heads_kv, group_size, HD), key_block, value_block, None
    )
    full_num = jnp.zeros((device_count, row_count, heads_kv * group_size * HD), jnp.float32)
    full_num = full_num.at[members].set(
        extra_num.reshape(GSIZE, row_count, heads_kv * group_size * HD)
    )
    full_den = jnp.zeros((device_count, row_count, heads_kv * group_size), jnp.float32)
    full_den = full_den.at[members].set(extra_den.reshape(GSIZE, row_count, heads_kv * group_size))
    got_num, got_den = (
        lax.psum_scatter(
            full_num.reshape(device_count * row_count, -1), "req", scatter_dimension=0, tiled=True
        ),
        lax.psum_scatter(
            full_den.reshape(device_count * row_count, -1), "req", scatter_dimension=0, tiled=True
        ),
    )
    numerator = numerator + got_num.reshape(numerator.shape)
    denominator = denominator + got_den.reshape(denominator.shape)
    attended = numerator / denominator[..., None]
    attended = jnp.where(live_rows[:, None, None, None], attended, 0.0).astype(jnp.bfloat16)
    return (
        attended.reshape(row_count, heads_query * HD),
        key_rows.reshape(row_count, heads_kv * HD),
        value_rows,
    )


def solution(mesh):
    in_specs = (
        P("req", "tp"),
        P(),
        P(None, "tp"),
        P(None, "tp"),
        P(None, "tp"),
        P("req", None, "tp"),
        P(),
        P(),
        P(),
    )
    out_specs = (P("req", "tp"), P("req", "tp"), P("req", "tp"))
    return jax.shard_map(body, mesh=mesh, in_specs=in_specs, out_specs=out_specs, check_vma=False)
```

profile of v0, /device:TPU:8, one launch (start us, length us, event | category | flops | bytes accessed | tf_op | source)
XLA Modules:
  0.0 566.9 jit_solution(6024013331039307176)
XLA Ops:
  7.2 0.7 all-gather.3.cloned.1.call-update
  8.0 1.2 multiply_cosine_fusion
  9.2 84.1 %all-gather.3.cloned.1.call-done = bf16[256,4608]{0,1:T(8,128)(2,1)} async-done(((bf16[256,576]{0,1:T(8,128)(2,1)}), bf16[256,4608]{0,1:T(8,128)(2,1)}) %all-gather.3.cloned.1.call-update) | async-done | bytes 2359312 | tf_op jit(solution)/shard_map/all_gather | solution.py:57
  93.3 2.3 fusion.1
  95.6 5.6 fusion.30
  101.3 1.0 copy.140
  102.2 1.0 copy.139
  103.3 1.3 multiply_subtract_fusion
  104.6 0.8 copy-done.2
  105.4 0.9 fusion.16
  106.4 1.8 copy.106
  108.4 1.8 fusion.35
  110.2 1.9 copy.141
  112.1 1.2 copy.142
  114.1 0.6 compare_convert_fusion
  114.8 1.6 sort.17
  116.4 73.9 %all-gather.5.cloned.1.call-done = bf16[8192,512]{0,1:T(8,128)(2,1)} async-done(((bf16[256,512]{0,1:T(8,128)(2,1)}), bf16[8192,512]{0,1:T(8,128)(2,1)}) %all-gather.5.cloned.1.call-update) | async-done | bytes 8388624 | tf_op jit(solution)/shard_map/all_gather | solution.py:86
  190.3 9.5 %copy.143 = bf16[64,8,32,256]{3,2,1,0:T(8,128)(2,1)} copy(bf16[64,8,32,256]{3,1,2,0:T(8,128)(2,1)} %bitcast.85) | data formatting | bytes 16777216
  199.9 14.6 %copy.107 = bf16[32,256,2,2,128]{4,1,3,2,0:T(8,128)(2,1)} copy(bf16[32,256,2,2,128]{1,0,4,3,2:T(8,128)(2,1)} %bitcast.83) | data formatting | bytes 16777216 | tf_op jit(solution)/shard_map/reshape | solution.py:92
  214.5 5.6 gather_fusion
  220.1 1.8 copy.108
  221.9 9.2 %bitcast_reduce_fusion = (f32[2,2,2048]{2,1,0:T(2,128)S(1)}, f32[2,2048,2,512]{1,3,2,0:T(8,128)}) fusion(bf16[2048,2,2,128]{3,0,2,1:T(8,128)(2,1)S(1)} %bitcast.86, bf16[512,2,128,1]{0,2,3,1:T(8,128)(2,1)} %bitcast.92), kind=kOutput, calls=%fused_computation.3 | convolution fusion | flops 1086316544 | bytes 19169280 | tf_op jit(solution)/shard_map/rkgd,ckd->kgrc/dot_general | solution.py:40
  231.1 0.7 scatter_fusion.1
  231.8 2.7 copy.134
  234.9 13.0 %fusion.4 = f32[2048,2,2,128]{3,0,2,1:T(8,128)} fusion(bf16[512,2,128,1]{0,2,3,1:T(8,128)(2,1)S(1)} %bitcast.90, f32[2,2048,2,512]{1,3,2,0:T(8,128)} %get-tuple-element.36), kind=kOutput, calls=%fused_computation.12 | convolution fusion | flops 1086324736 | bytes 21233664 | tf_op jit(solution)/shard_map/kgrc,ckd->rkgd/dot_general | solution.py:45
  247.8 8.7 %copy.133 = f32[2048,2,2,128]{3,2,1,0:T(2,128)} copy(f32[2048,2,2,128]{3,0,2,1:T(8,128)} %fusion.4) | data formatting | bytes 8388608 | tf_op jit(solution)/shard_map/reshape | solution.py:101
  256.6 6.4 %reshape.187 = f32[8,256,512]{2,1,0:T(8,128)} reshape(f32[2048,2,2,128]{3,2,1,0:T(2,128)} %copy.133) | data formatting | bytes 8388608 | tf_op jit(solution)/shard_map/reshape | solution.py:101
  263.0 7.9 %broadcast_in_dim.81 = f32[32,256,512]{2,1,0:T(8,128)} broadcast(f32[]{:T(128)} %constant.6.clone.1), dimensions={} | broadcast | bytes 16777220 | tf_op jit(solution)/shard_map/broadcast_in_dim | solution.py:99
  270.9 8.0 %scatter_fusion = f32[32,256,512]{2,1,0:T(8,128)} fusion(f32[32,256,512]{2,1,0:T(8,128)} %broadcast_in_dim.81, s32[8]{0:T(128)S(1)} %compare_select_fusion, f32[8,256,512]{2,1,0:T(8,128)} %reshape.187), kind=kCustom, calls=%fused_computation.1 | custom fusion | bytes 12582944 | tf_op jit(solution)/shard_map/scatter | solution.py:100
  278.9 17.5 %copy.116 = f32[8192,512]{0,1:T(8,128)} copy(f32[8192,512]{1,0:T(8,128)} %bitcast.82) | data formatting | bytes 33554432 | tf_op jit(solution)/shard_map/reshape | solution.py:107
  297.6 0.6 iota_compare_fusion.1
  298.3 0.6 iota_compare_fusion
  298.9 3.2 fusion.14
  302.8 0.8 copy.121
  303.5 4.0 fusion.32
  307.5 0.7 fusion.37
  308.2 1.7 copy.138
  310.0 1.7 copy.137
  311.7 1.1 multiply_subtract_fusion.1
  313.0 0.8 copy.118
  313.7 1.6 fusion.19
  315.3 1.7 copy.120
  317.0 2.3 fusion.38
  319.2 67.6 %reduce-scatter.7.cloned.1.call-done = f32[256,4]{1,0:T(8,128)} async-done(((f32[8192,4]{1,0:T(8,128)}), f32[256,4]{1,0:T(8,128)}) %reduce-scatter.7.cloned.1.call-update) | async-done | bytes 4112
  386.9 1.0 copy.135
  387.9 170.1 %reduce-scatter.5.cloned.1.call-done = f32[256,512]{0,1:T(8,128)} async-done(((f32[8192,512]{0,1:T(8,128)}), f32[256,512]{0,1:T(8,128)}) %reduce-scatter.5.cloned.1.call-update) | async-done | bytes 524304 | tf_op jit(solution)/shard_map/reduce_scatter | solution.py:106
  558.0 1.5 fusion.13
  559.5 0.8 copy.119
  (40 shorter events, 3.5 us)
Async XLA Ops:
  7.2 291.8 %copy-start = (bf16[4608,256]{1,0:T(8,128)(2,1)S(1)}, bf16[4608,256]{1,0:T(8,128)(2,1)}, u32[]{:S(2)}) copy-start(bf16[4608,256]{1,0:T(8,128)(2,1)} %param.13) | copy-start | bytes 7077892
  7.2 86.1 %all-gather.3.cloned.1.call-start = ((), (), s32[]{:S(2)}) async-start(), calls=%async_computation.2 | async-start | bytes 2654208 | tf_op jit(solution)/shard_map/all_gather | solution.py:57
  7.9 182.4 %all-gather.5.cloned.1.call-start = ((), (), s32[]{:S(2)}) async-start(), calls=%async_computation.3 | async-start | bytes 8650752 | tf_op jit(solution)/shard_map/all_gather | solution.py:86
  101.2 7.2 %copy-start.1 = (bf16[512,2,256]{2,1,0:T(2,128)(2,1)S(1)}, bf16[512,2,256]{2,1,0:T(2,128)(2,1)}, u32[]{:S(2)}) copy-start(bf16[512,2,256]{2,1,0:T(2,128)(2,1)} %param.14) | copy-start | bytes 1572868
  101.2 12.1 %copy-start.5 = (s32[4,8]{1,0:T(4,128)S(1)}, s32[4,8]{1,0:T(4,128)}, u32[]{:S(2)}) copy-start(s32[4,8]{1,0:T(4,128)} %param.16) | copy-start | bytes 388
  101.2 12.9 %copy-start.7 = (s32[32]{0:T(128)S(1)}, s32[32]{0:T(128)}, u32[]{:S(2)}) copy-start(s32[32]{0:T(128)} %param.15) | copy-start | bytes 388
  104.6 0.8 copy-start.2
  108.2 278.7 %reduce-scatter.7.cloned.1.call-start = ((), (), s32[]{:S(2)}) async-start(), calls=%async_computation.5 | async-start | bytes 4325376
  234.6 323.4 %reduce-scatter.5.cloned.1.call-start = ((), (), s32[]{:S(2)}) async-start(), calls=%async_computation.4 | async-start | bytes 17301504 | tf_op jit(solution)/shard_map/reduce_scatter | solution.py:106
  296.4 0.7 copy-start.8
  296.4 2.5 copy-start.6
  302.1 0.6 copy-start.4
  303.5 13.4 %copy-start.3 = (f32[256,4,64]{2,0,1:T(8,128)S(1)}, f32[256,4,64]{2,0,1:T(8,128)}, u32[]{:S(2)}) copy-start(f32[256,4,64]{2,0,1:T(8,128)} %copy-done.2) | copy-start | bytes 786436
Sparse Core Ops, SparseCore 0:
  10.6 82.6 all-gather.2
  108.3 82.0 all-gather.4
  234.7 152.1 reduce-scatter.6
  389.3 168.6 reduce-scatter.4
where the time goes:
time: 568 us; the launch traced here: 567 us
  waiting for transfers between devices  397 us (70%)
  local copies, waits for them, and re-layouts  104 us (18%)
  matrix products  38.6 us (7%)
  between operations  14 us (2%)
  other arithmetic  12.9 us (2%)
    reduce_scatter x1, waiting for transfers between devices, body(): lax.psum_scatter(full_num.reshape(device_count * row_count, -1), 'req', s...  170 us
    all_gather x1, waiting for transfers between devices, body(): gathered = lax.all_gather(hidden, 'tp', axis=1, tiled=True)  84.1 us
    all_gather x1, waiting for transfers between devices, body(): everyone = lax.all_gather(flat_query, 'req', axis=0, tiled=True)  73.9 us
    unnamed x5, waiting for transfers between devices  68.4 us
    unnamed x30, local copies, waits for them, and re-layouts  27.2 us
    reshape x1, local copies, waits for them, and re-layouts, body(): full_num.reshape(device_count * row_count, -1)  17.5 us
    reshape x2, local copies, waits for them, and re-layouts, body(): extra_num.reshape(GSIZE, row_count, heads_kv * group_size * HD)  15.2 us
    reshape x1, local copies, waits for them, and re-layouts, body(): everyone.reshape(device_count, row_count, heads_kv, group_size, HD)[members]  14.6 us
  transfers between devices with their start and end apart: 4, of which 4 were waited for; matrix products, arithmetic and copies ran while one was open for 16% of the time, Pallas kernels for 0%

commit v1 on v0

--- a/solution.py
+++ b/solution.py
@@ -54,7 +54,8 @@
 def body(hidden, norm_gain, w_query, w_key, w_value, prefix_kv, group_of, block_owner, lengths):
     device = lax.axis_index("req")
     row_count = hidden.shape[0]
-    gathered = lax.all_gather(hidden, "tp", axis=1, tiled=True)
+    repeated = jnp.stack([hidden] * lax.axis_size("tp"))
+    gathered = jnp.concatenate(lax.all_to_all(repeated, "tp", 0, 0), axis=1)
     features = gathered.astype(jnp.float32)
     row_scale = lax.rsqrt(jnp.mean(features * features, axis=1, keepdims=True) + EPSILON)
     normed = (features * row_scale * norm_gain[None, :]).astype(jnp.bfloat16)

time: 568 us -> 547 us (0.963)
  waiting for transfers between devices: 397 us -> 365 us
  starting transfers between devices: 0.56 us -> 11.8 us
  matrix products: 38.6 us -> 31.8 us
    all_gather x1 -> x0, waiting for transfers between devices: 84.1 us -> none  [body(): gathered = lax.all_gather(hidden, 'tp', axis=1, tiled=True)]
    all_to_all x0 -> x1, waiting for transfers between devices: none -> 33 us  [body(): gathered = jnp.concatenate(lax.all_to_all(repeated, 'tp', 0, 0), axis=1)]
    all_gather x1, waiting for transfers between devices: 73.9 us -> 90.6 us  [body(): everyone = lax.all_gather(flat_query, 'req', axis=0, tiled=True)]
    all_to_all x0 -> x1, starting transfers between devices: none -> 11.5 us  [body(): gathered = jnp.concatenate(lax.all_to_all(repeated, 'tp', 0, 0), axis=1)]
    dot_general x0 -> x2, local copies, waits for them, and re-layouts: none -> 11 us  [the longest x1 6.7 us: body(): query_raw = jnp.dot(normed, w_query, preferred_element_type=jnp.float32)]
    unnamed x30 -> x28, local copies, waits for them, and re-layouts: 27.2 us -> 19.4 us
    unnamed x5 -> x4, waiting for transfers between devices: 68.4 us -> 70.8 us
  transfers between devices with their start and end apart: 4 -> 4, of which waited for: 4 -> 4; matrix products, arithmetic and copies ran while one was open for 16% -> 18% of each run, Pallas kernels for 0% -> 0%
where the time goes in v1:
time: 547 us; the launch traced here: 545 us
  waiting for transfers between devices  365 us (67%)
  local copies, waits for them, and re-layouts  109 us (20%)
  matrix products  31.8 us (6%)
  between operations  14 us (3%)
  other arithmetic  13.3 us (2%)
  starting transfers between devices  11.8 us (2%)
    reduce_scatter x1, waiting for transfers between devices, body(): lax.psum_scatter(full_num.reshape(device_count * row_count, -1), 'req', s...  171 us
    all_gather x1, waiting for transfers between devices, body(): everyone = lax.all_gather(flat_query, 'req', axis=0, tiled=True)  90.6 us
    unnamed x4, waiting for transfers between devices  70.8 us
    all_to_all x1, waiting for transfers between devices, body(): gathered = jnp.concatenate(lax.all_to_all(repeated, 'tp', 0, 0), axis=1)  33 us
    unnamed x28, local copies, waits for them, and re-layouts  19.4 us
    reshape x1, local copies, waits for them, and re-layouts, body(): full_num.reshape(device_count * row_count, -1)  17.5 us
    reshape x2, local copies, waits for them, and re-layouts, body(): extra_num.reshape(GSIZE, row_count, heads_kv * group_size * HD)  15.2 us
    reshape x1, local copies, waits for them, and re-layouts, body(): everyone.reshape(device_count, row_count, heads_kv, group_size, HD)[members]  14.6 us
  transfers between devices with their start and end apart: 4, of which 4 were waited for; matrix products, arithmetic and copies ran while one was open for 18% of the time, Pallas kernels for 0%

profile of v1, /device:TPU:8, one launch (start us, length us, event | category | flops | bytes accessed | tf_op | source)
XLA Modules:
  0.0 545.5 jit_solution(9373684520356153828)
XLA Ops:
  7.2 2.7 stack.2
  9.9 11.5 %all-to-all-start = ((bf16[8,256,576]{1,2,0:T(8,128)(2,1)}), bf16[8,256,576]{1,2,0:T(8,128)(2,1)}, u32[]{:S(2)}, u32[]{:S(2)}) async-start(bf16[8,256,576]{1,2,0:T(8,128)(2,1)} %stack.2), calls=%async_computation | async-start | bytes 4718592 | tf_op jit(solution)/shard_map/all_to_all | solution.py:58
  21.5 6.7 %copy.100 = bf16[512,4608]{1,0:T(8,128)(2,1)} copy(bf16[512,4608]{0,1:T(8,128)(2,1)} %bitcast.105) | data formatting | bytes 9437184 | tf_op jit(solution)/shard_map/dot_general | solution.py:65
  28.2 0.3 multiply_cosine_fusion
  28.6 33.0 %all-to-all-done = bf16[8,256,576]{1,2,0:T(8,128)(2,1)} async-done(((bf16[8,256,576]{1,2,0:T(8,128)(2,1)}), bf16[8,256,576]{1,2,0:T(8,128)(2,1)}, u32[]{:S(2)}, u32[]{:S(2)}) %all-to-all-start) | async-done | bytes 2359328 | tf_op jit(solution)/shard_map/all_to_all | solution.py:58
  61.6 2.5 multiply_reduce_fusion
  64.0 2.1 multiply_convert_fusion
  66.1 1.4 fusion.32
  67.6 0.7 fusion.15
  68.5 3.2 fusion.29
  71.6 1.9 copy.109
  73.5 1.2 copy.110
  74.9 0.6 select_reduce_fusion
  75.6 0.6 compare_convert_fusion
  76.2 1.6 sort.17
  77.8 90.6 %all-gather.2.cloned.1.call-done = bf16[8192,512]{0,1:T(8,128)(2,1)} async-done(((bf16[256,512]{0,1:T(8,128)(2,1)}), bf16[8192,512]{0,1:T(8,128)(2,1)}) %all-gather.2.cloned.1.call-update) | async-done | bytes 8388624 | tf_op jit(solution)/shard_map/all_gather | solution.py:87
  168.4 9.5 %copy.111 = bf16[64,8,32,256]{3,2,1,0:T(8,128)(2,1)} copy(bf16[64,8,32,256]{3,1,2,0:T(8,128)(2,1)} %bitcast.104) | data formatting | bytes 16777216
  177.9 14.6 %copy.73 = bf16[32,256,2,2,128]{4,1,3,2,0:T(8,128)(2,1)} copy(bf16[32,256,2,2,128]{1,0,4,3,2:T(8,128)(2,1)} %bitcast.102) | data formatting | bytes 16777216 | tf_op jit(solution)/shard_map/reshape | solution.py:93
  192.5 5.6 %gather_fusion = bf16[8,256,2,2,128]{4,1,3,2,0:T(8,128)(2,1)} fusion(bf16[32,256,2,2,128]{4,1,3,2,0:T(8,128)(2,1)} %copy.73, s32[1024]{0:T(1024)S(1)} %pad_clamp_fusion), kind=kCustom, calls=%fused_computation | custom fusion | bytes 4194336 | tf_op jit(solution)/shard_map/gather | solution.py:93
  198.1 1.8 copy.74
  199.9 9.2 %bitcast_reduce_fusion = (f32[2,2,2048]{2,1,0:T(2,128)S(1)}, f32[2,2048,2,512]{1,3,2,0:T(8,128)}) fusion(bf16[2048,2,2,128]{3,0,2,1:T(8,128)(2,1)S(1)} %bitcast.113, bf16[512,2,128,1]{0,2,3,1:T(8,128)(2,1)} %bitcast.116), kind=kOutput, calls=%fused_computation.3 | convolution fusion | flops 1086316544 | bytes 19169280 | tf_op jit(solution)/shard_map/rkgd,ckd->kgrc/dot_general | solution.py:40
  209.1 0.7 scatter_fusion.1
  209.9 2.7 copy.106
  212.6 0.2 reduce-scatter.5.cloned.1.call-start
  212.9 13.0 %fusion.3 = f32[2048,2,2,128]{3,0,2,1:T(8,128)} fusion(bf16[512,2,128,1]{0,2,3,1:T(8,128)(2,1)S(1)} %bitcast.115, f32[2,2048,2,512]{1,3,2,0:T(8,128)} %get-tuple-element.26), kind=kOutput, calls=%fused_computation.12 | convolution fusion | flops 1086324736 | bytes 21233664 | tf_op jit(solution)/shard_map/kgrc,ckd->rkgd/dot_general | solution.py:45
  225.8 8.7 %copy.105 = f32[2048,2,2,128]{3,2,1,0:T(2,128)} copy(f32[2048,2,2,128]{3,0,2,1:T(8,128)} %fusion.3) | data formatting | bytes 8388608 | tf_op jit(solution)/shard_map/reshape | solution.py:102
  234.6 6.4 %reshape.212 = f32[8,256,512]{2,1,0:T(8,128)} reshape(f32[2048,2,2,128]{3,2,1,0:T(2,128)} %copy.105) | data formatting | bytes 8388608 | tf_op jit(solution)/shard_map/reshape | solution.py:102
  241.0 7.9 %broadcast_in_dim.81 = f32[32,256,512]{2,1,0:T(8,128)} broadcast(f32[]{:T(128)} %constant.6.clone.1), dimensions={} | broadcast | bytes 16777220 | tf_op jit(solution)/shard_map/broadcast_in_dim | solution.py:100
  248.9 8.0 %scatter_fusion = f32[32,256,512]{2,1,0:T(8,128)} fusion(f32[32,256,512]{2,1,0:T(8,128)} %broadcast_in_dim.81, s32[8]{0:T(128)S(1)} %compare_select_fusion, f32[8,256,512]{2,1,0:T(8,128)} %reshape.212), kind=kCustom, calls=%fused_computation.1 | custom fusion | bytes 12582944 | tf_op jit(solution)/shard_map/scatter | solution.py:101
  256.9 17.5 %copy.82 = f32[8192,512]{0,1:T(8,128)} copy(f32[8192,512]{1,0:T(8,128)} %bitcast.101) | data formatting | bytes 33554432 | tf_op jit(solution)/shard_map/reshape | solution.py:108
  274.4 4.3 copy.96
  278.7 0.6 dynamic_slice.3
  279.3 0.6 iota_compare_fusion.1
  280.0 0.6 iota_compare_fusion
  280.6 3.2 fusion.2
  283.9 1.1 fusion.13
  285.0 0.8 copy.86
  285.8 3.2 fusion.31
  289.0 0.6 copy-done.3
  289.7 0.8 copy.85
  290.4 1.0 copy.70
  291.5 0.2 copy.69
  291.7 2.5 fusion.30
  294.2 70.7 %reduce-scatter.7.cloned.1.call-done = f32[256,4]{1,0:T(8,128)} async-done(((f32[8192,4]{1,0:T(8,128)}), f32[256,4]{1,0:T(8,128)}) %reduce-scatter.7.cloned.1.call-update) | async-done | bytes 4112
  364.9 1.0 copy.107
  365.9 170.8 %reduce-scatter.5.cloned.1.call-done = f32[256,512]{0,1:T(8,128)} async-done(((f32[8192,512]{0,1:T(8,128)}), f32[256,512]{0,1:T(8,128)}) %reduce-scatter.5.cloned.1.call-update) | async-done | bytes 524304 | tf_op jit(solution)/shard_map/reduce_scatter | solution.py:107
  536.7 1.4 fusion.12
  538.1 0.8 copy.84
  (41 shorter events, 0.6 us)
Async XLA Ops:
  7.2 276.7 %copy-start = (bf16[4608,256]{1,0:T(8,128)(2,1)S(1)}, bf16[4608,256]{1,0:T(8,128)(2,1)}, u32[]{:S(2)}) copy-start(bf16[4608,256]{1,0:T(8,128)(2,1)} %param.13) | copy-start | bytes 7077892
  7.2 14.3 %copy-start.6 = (f32[4608]{0:T(1024)S(1)}, f32[4608]{0:T(1024)}, u32[]{:S(2)}) copy-start(f32[4608]{0:T(1024)} %param.10) | copy-start | bytes 55300
  9.9 51.7 %all-to-all-start = ((bf16[8,256,576]{1,2,0:T(8,128)(2,1)}), bf16[8,256,576]{1,2,0:T(8,128)(2,1)}, u32[]{:S(2)}, u32[]{:S(2)}) async-start(bf16[8,256,576]{1,2,0:T(8,128)(2,1)} %stack.2), calls=%async_computation | async-start | bytes 4718592 | tf_op jit(solution)/shard_map/all_to_all | solution.py:58
  21.4 146.9 %all-gather.2.cloned.1.call-start = ((), (), s32[]{:S(2)}) async-start(), calls=%async_computation.3 | async-start | bytes 8650752 | tf_op jit(solution)/shard_map/all_gather | solution.py:87
  61.6 4.6 copy-start.1
  66.1 1.5 copy-start.2
  67.5 7.3 %copy-start.7 = (s32[4,8]{1,0:T(4,128)S(1)}, s32[4,8]{1,0:T(4,128)}, u32[]{:S(2)}) copy-start(s32[4,8]{1,0:T(4,128)} %param.16) | copy-start | bytes 388
  67.5 8.0 %copy-start.8 = (s32[32]{0:T(128)S(1)}, s32[32]{0:T(128)}, u32[]{:S(2)}) copy-start(s32[32]{0:T(128)} %param.15) | copy-start | bytes 388
  68.4 296.5 %reduce-scatter.7.cloned.1.call-start = ((), (), s32[]{:S(2)}) async-start(), calls=%async_computation.5 | async-start | bytes 4325376
  212.6 324.0 %reduce-scatter.5.cloned.1.call-start = ((), (), s32[]{:S(2)}) async-start(), calls=%async_computation.4 | async-start | bytes 17301504 | tf_op jit(solution)/shard_map/reduce_scatter | solution.py:107
  274.4 4.3 copy-start.9
  285.0 4.0 copy-start.4
  289.0 0.6 copy-start.3
  289.6 247.0 %copy-start.5 = (bf16[256,256]{0,1:T(8,128)(2,1)S(1)}, bf16[256,256]{0,1:T(8,128)(2,1)}, u32[]{:S(2)}) copy-start(bf16[256,256]{0,1:T(8,128)(2,1)} %copy-done.4) | copy-start | bytes 393220
Sparse Core Ops, SparseCore 0:
  68.5 99.8 all-gather.1
  212.7 152.1 reduce-scatter.6
  367.5 169.1 reduce-scatter.4
